TPU v7x, 32 devices: a whole 2x2x4 slice. The times are simulated.
32 devices in a mesh: sec: 8 (over y, x, core), term: 4 (over z).
Axes of the slice: x: 2, y: 2, z: 4, core: 2. Of those that a mesh axis runs over, the one named last changes fastest.
Arguments:
- meet_env: bfloat16 [8, 24, 256, 256], P('sec', 'term'), may hold values from -0.375 to 0.375
- meet_iso: bfloat16 [8, 256, 2, 256], P('sec'), may hold values from -0.3125 to 0.3125
- last_site: bfloat16 [8, 256, 2, 256], P('sec'), may hold values from -60 to 60
- first_site: bfloat16 [8, 256, 2, 256], P('sec'), may hold values from -0.375 to 0.375
- term_kind: int32 [24, 2], P('term'), may hold values from 0 to 3
Outputs:
- two_site_out: float32 [8, 256, 2, 2, 256], P('sec')
All inputs are finite; a program needn't handle non-finite values.
Results may differ from a plain program's by a relative error of at most 0.013.
Values may be sent and summed in bfloat16 or wider, within the bound.
A program may use at most 64 MiB of HBM per device.

v0:
```python
import functools

import jax
import jax.numpy as jnp
from jax import lax
from jax.experimental import pallas as pl
from jax.experimental.pallas import tpu as pltpu
from jax.sharding import PartitionSpec as P

PHYS = 2
STEPS = 2
PARTS = 4
LAG = 9
GROUP = 2
step_size = 0.2
epsilon = 1e-06
F32 = jnp.float32
BF16 = jnp.bfloat16
MESH = pl.DeviceIdType.MESH


def matmul(lhs, rhs):
    return jnp.dot(lhs, rhs, preferred_element_type=F32)


def kernel(
    n_sec,
    n_term,
    terms,
    kind_ref,
    env_ref,
    iso_ref,
    last_ref,
    first_ref,
    out_ref,
    envbuf,
    rbuf,
    fresh,
    piso,
    came,
    basis,
    table,
    h,
    v,
    two_site,
    early,
    acc,
    tot,
    recv,
    one_send,
    one_recv,
    env_send,
    env_recv,
    fresh_send,
    fresh_recv,
    in_send,
    chunk_recv,
    out_send,
):
    pairs = PHYS * PHYS
    sec = lax.axis_index("sec")
    term = lax.axis_index("term")
    odd = lax.rem(sec, 2)
    is_odd = odd == 1
    is_even = odd == 0
    partner = sec + 1 - 2 * odd
    following = lax.rem(sec + 1, n_sec)
    before = lax.rem(sec + n_sec - 1, n_sec)
    half = n_term // 2
    left_side = term < half
    inward = jnp.where(left_side, term + 1, term - 1)
    outward = jnp.where(left_side, term - 1, term + 1)
    has_outward = jnp.logical_and(term > 0, term < n_term - 1)
    middle = jnp.logical_or(term == half - 1, term == half)
    in_slot = jnp.where(middle, 1, 0)

    def at(s, t):
        return dict(device_id=(s, t), device_id_type=MESH)

    barrier = pltpu.get_barrier_semaphore()
    for s in (following, before):
        pl.semaphore_signal(barrier, inc=1, **at(s, term))
    pl.semaphore_signal(barrier, inc=1, **at(sec, inward))

    @pl.when(has_outward)
    def _():
        pl.semaphore_signal(barrier, inc=1, **at(sec, outward))
        pl.semaphore_wait(barrier, 4)

    @pl.when(jnp.logical_not(has_outward))
    def _():
        pl.semaphore_wait(barrier, 3)

    def remote(src, dst, send, receive, s, t):
        return pltpu.make_async_remote_copy(
            src_ref=src, dst_ref=dst, send_sem=send, recv_sem=receive, **at(s, t)
        )

    iso_copy = remote(iso_ref, piso, one_send.at[0], one_recv.at[0], partner, term)
    last_copy = remote(last_ref, came, one_send.at[1], one_recv.at[1], following, term)

    def env_copy(k):
        return remote(
            env_ref.at[k], envbuf.at[odd, k], env_send.at[k], env_recv.at[k], partner, term
        )

    def fresh_copy(k):
        return remote(
            fresh.at[k], envbuf.at[0, k], fresh_send.at[k], fresh_recv.at[k], following, term
        )

    def in_copy(n, x):
        return remote(
            acc.at[n, x],
            recv.at[n, in_slot, x],
            in_send.at[n, x],
            chunk_recv.at[n, in_slot, x],
            sec,
            inward,
        )

    def out_copy(n, x):
        return remote(
            tot.at[n, x],
            recv.at[n, 1, x],
            out_send.at[n, x],
            chunk_recv.at[n, 1, x],
            sec,
            outward,
        )

    def arrived(n, slot, x):
        return remote(
            acc.at[n, x],
            recv.at[n, slot, x],
            in_send.at[n, x],
            chunk_recv.at[n, slot, x],
            sec,
            inward,
        )

    iso_copy.start()
    for k in range(terms):
        env_copy(k).start()
    last_copy.start()

    def set_basis(which, source):
        @pl.when(is_odd)
        def _():
            for s in range(PHYS):
                value = source[s]
                turned = value.T
                basis[which, s] = value
                table[which, s] = turned
                if s == 1:
                    table[which, 2] = -turned

        @pl.when(is_even)
        def _():
            for s in range(PHYS):
                value = source[s]
                basis[which, s] = value.T
                table[which, s] = value
                if s == 1:
                    table[which, 2] = -value

    set_basis(1, iso_ref)

    @pl.when(is_odd)
    def _():
        def turn(k, carry):
            rbuf[k] = env_ref[k].T
            return carry

        lax.fori_loop(0, terms, turn, 0)

    iso_copy.wait_recv()
    set_basis(0, piso)

    def extend(values, which, kinds):
        wide = [
            [matmul(value, basis[which, r]).astype(BF16) for r in range(PHYS)] for value in values
        ]
        results = []
        for (wide_0, wide_1), kind in zip(wide, kinds):
            first = jnp.where(kind == 1, 1, jnp.where(kind == 3, 2, 0))
            second = jnp.where(kind == 0, 1, jnp.where(kind == 2, 2, 0))
            result = matmul(table[which, first], wide_0) + matmul(table[which, second], wide_1)
            results.append(result.astype(BF16))
        return results

    group = GROUP if terms % GROUP == 0 else 1

    def extend_group(i, carry):
        members = [group * i + m for m in range(group)]
        for k in members:
            env_copy(k).wait_recv()
        kinds = [kind_ref[k, 1 - odd] for k in members]
        values = extend([envbuf[1 - odd, k] for k in members], 0, kinds)
        values = extend(values, 1, kinds)

        @pl.when(is_odd)
        def _():
            for k, value in zip(members, values):
                fresh[k] = value
                fresh_copy(k).start()

        @pl.when(is_even)
        def _():
            for k, value in zip(members, values):
                rbuf[k] = value.T

        return carry

    lax.fori_loop(0, terms // group, extend_group, 0)

    last_copy.wait_recv()
    for s in range(PHYS):
        for t in range(PHYS):
            value = matmul(came[s], first_ref[t])
            two_site[PHYS * s + t] = value
            v[PHYS * s + t] = value.astype(BF16)

    def right_of(n, x):
        value = v[x]
        for k in range(terms):
            h[n, k, x] = matmul(value, rbuf[k]).astype(BF16)

    def first_right(x, carry):
        right_of(0, x)
        return carry

    lax.fori_loop(0, pairs, first_right, 0)

    def term_of(n, k, x):
        s = x // PHYS
        t = lax.rem(x, PHYS)
        kind_0, kind_1 = kind_ref[k, 0], kind_ref[k, 1]
        flip_0, minus_0 = lax.rem(kind_0, 2), kind_0 // 2
        flip_1, minus_1 = lax.rem(kind_1, 2), kind_1 // 2
        from_s = s + flip_0 - 2 * s * flip_0
        from_t = t + flip_1 - 2 * t * flip_1
        sign = (1 - 2 * s * minus_0) * (1 - 2 * t * minus_1)
        value = h[n, k, PHYS * from_s + from_t] * sign.astype(F32).astype(BF16)
        return matmul(envbuf[0, k], value)

    @pl.when(is_even)
    def _():
        for x in range(pairs):
            early[x] = jnp.zeros(early.shape[1:], F32)

        def early_term(k, carry):
            fresh_copy(k).wait_recv()
            for x in range(pairs):
                early[x] += term_of(0, k, x)
            return carry

        lax.fori_loop(0, terms - 1, early_term, 0)
        fresh_copy(terms - 1).wait_recv()

    rows = two_site.shape[1] // PARTS
    chunks = pairs * PARTS

    def put_partial(n, x, total):
        total = total.astype(BF16)
        for part in range(PARTS):
            acc[n, PARTS * x + part] = total[part * rows : (part + 1) * rows]

    def full_partial(n, x):
        total = term_of(n, 0, x)
        for k in range(1, terms):
            total = total + term_of(n, k, x)
        put_partial(n, x, total)

    def partial_of(n, x):
        if n > 0:
            full_partial(n, x)
            return

        @pl.when(is_odd)
        def _():
            full_partial(n, x)

        @pl.when(is_even)
        def _():
            put_partial(n, x, early[x] + term_of(n, terms - 1, x))

    def pass_inward(n, j):
        @pl.when(has_outward)
        def _():
            arrived(n, 0, j).wait_recv()
            acc[n, j] = (acc[n, j].astype(F32) + recv[n, 0, j].astype(F32)).astype(BF16)

        in_copy(n, j).start()

    def pass_outward(n, j, squares):
        arrived(n, 1, j).wait_recv()
        came_in = recv[n, 1, j].astype(F32)
        own = jnp.where(middle, 1.0, 0.0)
        whole = (came_in + own * acc[n, j].astype(F32)).astype(BF16)

        @pl.when(has_outward)
        def _():
            tot[n, j] = whole
            out_copy(n, j).start()

        x = j // PARTS
        span = pl.ds(pl.multiple_of(lax.rem(j, PARTS) * rows, rows), rows)
        value = two_site[x, span] - step_size * whole.astype(F32)
        two_site[x, span] = value
        if n < STEPS - 1:
            v[x, span] = value.astype(BF16)
            return squares
        return squares + jnp.sum((value * value).reshape((rows // 8, 8, value.shape[1])), axis=0)

    lag = jnp.where(has_outward, min(LAG, chunks), chunks)
    zero = jnp.zeros((8, two_site.shape[2]), F32)
    for n in range(STEPS):

        def step(j, squares):
            @pl.when(jnp.logical_and(j < chunks, lax.rem(j, PARTS) == 0))
            def _():
                partial_of(n, j // PARTS)

            @pl.when(j < chunks)
            def _():
                pass_inward(n, j)

            return squares

        def head(j, squares):
            return step(j, squares)

        def body(j, squares):
            squares = step(j, squares)
            done = j - lag
            squares = pass_outward(n, done, squares)
            if n < STEPS - 1:

                @pl.when(lax.rem(done, PARTS) == PARTS - 1)
                def _():
                    right_of(n + 1, done // PARTS)

            return squares

        lax.fori_loop(0, lag, head, 0)
        squares = lax.fori_loop(lag, chunks + lag, body, zero)

    size = two_site.shape[0] * two_site.shape[1] * two_site.shape[2]
    scale = lax.rsqrt(jnp.full((1, 1), jnp.sum(squares), F32) / size + epsilon)

    lanes = out_ref.shape[1]
    halves = two_site.shape[2] // lanes
    stride = PHYS * PHYS * halves
    for s in range(PHYS):
        for t in range(PHYS):
            for c in range(halves):
                span = pl.ds((s * halves + c) * PHYS + t, two_site.shape[1], stride=stride)
                columns = pl.ds(c * lanes, lanes)
                out_ref[span, :] = two_site[PHYS * s + t, :, columns] * scale

    iso_copy.wait_send()
    last_copy.wait_send()

    def drain_term(k, carry):
        env_copy(k).wait_send()

        @pl.when(is_odd)
        def _():
            fresh_copy(k).wait_send()

        return carry

    lax.fori_loop(0, terms, drain_term, 0)
    for n in range(STEPS):

        def drain_chunk(x, carry):
            in_copy(n, x).wait_send()

            @pl.when(has_outward)
            def _():
                out_copy(n, x).wait_send()

            return carry

        lax.fori_loop(0, chunks, drain_chunk, 0)


def shards(n_sec, n_term, meet_env, meet_iso, last_site, first_site, term_kind):
    terms, bond = meet_env.shape[1], meet_env.shape[2]
    pairs = PHYS * PHYS

    def by_level(site):
        return jnp.transpose(site[0], (1, 0, 2))

    vmem = pl.BlockSpec(memory_space=pltpu.VMEM)
    block = (bond, bond)
    chunks = pairs * PARTS
    strip = (bond // PARTS, bond)
    lanes = min(bond, 128)
    dma = pltpu.SemaphoreType.DMA
    out = pl.pallas_call(
        functools.partial(kernel, n_sec, n_term, terms),
        out_shape=jax.ShapeDtypeStruct((pairs * bond * bond // lanes, lanes), F32),
        in_specs=[pl.BlockSpec(memory_space=pltpu.SMEM)] + [vmem] * 4,
        out_specs=vmem,
        scratch_shapes=[
            pltpu.VMEM((2, terms) + block, BF16),
            pltpu.VMEM((terms,) + block, BF16),
            pltpu.VMEM((terms,) + block, BF16),
            pltpu.VMEM((PHYS,) + block, BF16),
            pltpu.VMEM((PHYS,) + block, BF16),
            pltpu.VMEM((2, PHYS) + block, BF16),
            pltpu.VMEM((2, 3) + block, BF16),
            pltpu.VMEM((STEPS, terms, pairs) + block, BF16),
            pltpu.VMEM((pairs,) + block, BF16),
            pltpu.VMEM((pairs,) + block, F32),
            pltpu.VMEM((pairs,) + block, F32),
            pltpu.VMEM((STEPS, chunks) + strip, BF16),
            pltpu.VMEM((STEPS, chunks) + strip, BF16),
            pltpu.VMEM((STEPS, 2, chunks) + strip, BF16),
            dma((2,)),
            dma((2,)),
            dma((terms,)),
            dma((terms,)),
            dma((terms,)),
            dma((terms,)),
            dma((STEPS, chunks)),
            dma((STEPS, 2, chunks)),
            dma((STEPS, chunks)),
        ],
        compiler_params=pltpu.CompilerParams(
            collective_id=0, has_side_effects=True, vmem_limit_bytes=48 * 1024 * 1024
        ),
    )(term_kind, meet_env[0], by_level(meet_iso), by_level(last_site), by_level(first_site))
    out = out.reshape(bond, PHYS, bond // lanes, PHYS, lanes)
    out = jnp.transpose(out, (0, 1, 3, 2, 4))
    return out.reshape(1, bond, PHYS, PHYS, bond)


def solution(mesh):
    in_specs = (
        P("sec", "term", None, None),
        P("sec", None, None, None),
        P("sec", None, None, None),
        P("sec", None, None, None),
        P("term", None),
    )
    out_specs = P("sec", None, None, None, None)
    body = functools.partial(shards, mesh.shape["sec"], mesh.shape["term"])
    return jax.shard_map(body, mesh=mesh, in_specs=in_specs, out_specs=out_specs, check_vma=False)
```

profile of v0, /device:TPU:0, one launch (start us, length us, event | category | flops | bytes accessed | tf_op | source)
XLA Modules:
  0.0 53.9 jit_solution(5011659342228483533)
XLA Ops:
  0.0 0.0 copy-start.3
  0.0 0.0 copy-start.1
  0.0 0.0 copy-start.2
  0.0 0.7 %copy-done.3 = s32[6,2]{0,1:T(2,128)S(1)} copy-done((s32[6,2]{0,1:T(2,128)S(1)}, s32[6,2]{0,1:T(2,128)}, u32[]{:S(2)}) %copy-start.3) | copy-done | bytes 72
  0.7 0.1 copy.9.kind_ref
  0.8 0.0 copy-start
  0.8 1.1 %copy.14 = bf16[1,256,2,256]{3,1,2,0:T(8,128)(2,1)S(1)} copy(bf16[1,256,2,256]{3,2,1,0:T(2,128)(2,1)} %param.6) | data formatting | bytes 524288 | tf_op args[1]
  1.8 0.0 copy-done.1
  1.8 0.0 copy-done.2
  1.8 0.1 copy_bitcast_fusion
  1.9 0.1 copy-done
  2.0 50.9 %shard_map.55 = f32[2048,128]{1,0:T(8,128)S(1)} custom-call(s32[6,2]{1,0:T(8,128)S(1)} %copy.9.kind_ref, bf16[6,256,256]{2,1,0:T(8,128)(2,1)S(1)} %bitcast.21, bf16[2,256,256]{2,1,0:T(8,128)(2,1)S(1)} %bitcast.20, bf16[2,256,256]{2,1,0:T(8,128)(2,1)S(1)} %get-tuple-element.6.last_ref, bf16[2,256,256]{2,1,0:T(8,128)(2,1)S(1)} %get-tuple-element.5.first_ref), custom_call_target="tpu_custom_call" | custom-call | tf_op jit(solution)/shard_map/pallas_call | solution.py:402
  52.9 1.0 %copy.16 = f32[1,256,2,2,256]{4,3,2,1,0:T(2,128)} copy(f32[1,256,2,2,256]{4,3,2,1,0:T(2,128)S(1)} %bitcast.19) | data formatting | bytes 2097152
Async XLA Ops:
  0.0 0.7 %copy-start.3 = (s32[6,2]{0,1:T(2,128)S(1)}, s32[6,2]{0,1:T(2,128)}, u32[]{:S(2)}) copy-start(s32[6,2]{0,1:T(2,128)} %param.9) | copy-start | bytes 148
  0.0 1.8 %copy-start.1 = (bf16[1,256,2,256]{3,2,1,0:T(2,128)(2,1)S(1)}, bf16[1,256,2,256]{3,2,1,0:T(2,128)(2,1)}, u32[]{:S(2)}) copy-start(bf16[1,256,2,256]{3,2,1,0:T(2,128)(2,1)} %param.8) | copy-start | bytes 786436
  0.0 1.8 %copy-start.2 = (bf16[1,256,2,256]{3,2,1,0:T(2,128)(2,1)S(1)}, bf16[1,256,2,256]{3,2,1,0:T(2,128)(2,1)}, u32[]{:S(2)}) copy-start(bf16[1,256,2,256]{3,2,1,0:T(2,128)(2,1)} %param.7) | copy-start | bytes 786436
  0.8 1.3 %copy-start = (bf16[1,6,256,256]{3,2,1,0:T(8,128)(2,1)S(1)}, bf16[1,6,256,256]{3,2,1,0:T(8,128)(2,1)}, u32[]{:S(2)}) copy-start(bf16[1,6,256,256]{3,2,1,0:T(8,128)(2,1)} %param.5) | copy-start | bytes 2359300
where the time goes:
time: 54.1 us; the launch traced here: 53.9 us
  Pallas kernels  50.9 us (94%)
  local copies, waits for them, and re-layouts  2.97 us (5%)
    pallas_call x1, Pallas kernels, shards(): pl.pallas_call(functools.partial(kernel, n_sec, n_term, terms), out_shape...  50.9 us
    unnamed x11, local copies, waits for them, and re-layouts  2.89 us

commit v1 on v0

v1 whole, which is shorter than its diff:
```python
import functools

import jax
import jax.numpy as jnp
from jax import lax
from jax.experimental import pallas as pl
from jax.experimental.pallas import tpu as pltpu
from jax.sharding import PartitionSpec as P

PHYS = 2
STEPS = 2
PARTS = 4
LAG = 9
GROUP = 2
step_size = 0.2
epsilon = 1e-06
F32 = jnp.float32
BF16 = jnp.bfloat16
MESH = pl.DeviceIdType.MESH


def matmul(lhs, rhs):
    return jnp.dot(lhs, rhs, preferred_element_type=F32)


def kernel(
    n_sec,
    n_term,
    terms,
    kind_ref,
    env_ref,
    iso_ref,
    last_ref,
    first_ref,
    out_ref,
    left,
    rbuf,
    mid,
    came_mid,
    fresh,
    piso,
    came,
    basis,
    table,
    h,
    v,
    two_site,
    acc,
    tot,
    recv,
    one_send,
    one_recv,
    mid_send,
    mid_recv,
    fresh_send,
    fresh_recv,
    in_send,
    chunk_recv,
    out_send,
):
    pairs = PHYS * PHYS
    rows = left.shape[1] // PARTS
    chunks = pairs * PARTS
    sec = lax.axis_index("sec")
    term = lax.axis_index("term")
    odd = lax.rem(sec, 2)
    is_odd = odd == 1
    is_even = odd == 0
    partner = sec + 1 - 2 * odd
    following = lax.rem(sec + 1, n_sec)
    before = lax.rem(sec + n_sec - 1, n_sec)
    ahead = lax.rem(sec + 2, n_sec)
    behind = lax.rem(sec + n_sec - 2, n_sec)
    half = n_term // 2
    left_side = term < half
    inward = jnp.where(left_side, term + 1, term - 1)
    outward = jnp.where(left_side, term - 1, term + 1)
    has_outward = jnp.logical_and(term > 0, term < n_term - 1)
    middle = jnp.logical_or(term == half - 1, term == half)
    in_slot = jnp.where(middle, 1, 0)

    def at(s, t):
        return dict(device_id=(s, t), device_id_type=MESH)

    barrier = pltpu.get_barrier_semaphore()
    pl.semaphore_signal(barrier, inc=1, **at(partner, term))
    pl.semaphore_signal(barrier, inc=1, **at(sec, inward))

    @pl.when(has_outward)
    def _():
        pl.semaphore_signal(barrier, inc=1, **at(sec, outward))

    @pl.when(is_odd)
    def _():
        pl.semaphore_signal(barrier, inc=1, **at(following, term))

    @pl.when(is_even)
    def _():
        for s in (ahead, behind, before):
            pl.semaphore_signal(barrier, inc=1, **at(s, term))

    def remote(src, dst, send, receive, s, t):
        return pltpu.make_async_remote_copy(
            src_ref=src, dst_ref=dst, send_sem=send, recv_sem=receive, **at(s, t)
        )

    iso_copy = remote(iso_ref, piso, one_send.at[0], one_recv.at[0], partner, term)
    last_copy = remote(last_ref, came, one_send.at[1], one_recv.at[1], following, term)
    env_copy = remote(env_ref, left, one_send.at[2], one_recv.at[2], partner, term)

    def mid_copy(k):
        return remote(mid.at[k], came_mid.at[k], mid_send.at[k], mid_recv.at[k], partner, term)

    def block_of(g):
        return pl.ds(pl.multiple_of(g * rows, rows), rows)

    def fresh_first(k):
        return remote(
            fresh.at[k, pl.ds(0, rows)],
            left.at[k, pl.ds(0, rows)],
            fresh_send.at[k],
            fresh_recv.at[k],
            ahead,
            term,
        )

    def fresh_block(g):
        return remote(
            fresh.at[:, block_of(g)],
            left.at[:, block_of(g)],
            fresh_send.at[terms - 1 + g],
            fresh_recv.at[terms - 1 + g],
            ahead,
            term,
        )

    def in_copy(n, x):
        return remote(
            acc.at[n, x],
            recv.at[n, in_slot, x],
            in_send.at[n, x],
            chunk_recv.at[n, in_slot, x],
            sec,
            inward,
        )

    def out_copy(n, x):
        return remote(
            tot.at[n, x],
            recv.at[n, 1, x],
            out_send.at[n, x],
            chunk_recv.at[n, 1, x],
            sec,
            outward,
        )

    def arrived(n, slot, x):
        return remote(
            acc.at[n, x],
            recv.at[n, slot, x],
            in_send.at[n, x],
            chunk_recv.at[n, slot, x],
            sec,
            inward,
        )

    def set_basis(which, source, flip):
        for s in range(PHYS):
            value = source[s]
            turned = value.T
            basis[which, s] = turned if flip else value
            table[which, s] = value if flip else turned
            if s == 1:
                table[which, 2] = -value if flip else -turned

    def extend(values, which, kinds):
        wide = [
            [matmul(value, basis[which, r]).astype(BF16) for r in range(PHYS)] for value in values
        ]
        results = []
        for (wide_0, wide_1), kind in zip(wide, kinds):
            first = jnp.where(kind == 1, 1, jnp.where(kind == 3, 2, 0))
            second = jnp.where(kind == 0, 1, jnp.where(kind == 2, 2, 0))
            result = matmul(table[which, first], wide_0) + matmul(table[which, second], wide_1)
            results.append(result.astype(BF16))
        return results

    group = GROUP if terms % GROUP == 0 else 1

    def own_group(i, carry):
        members = [group * i + m for m in range(group)]
        kinds = [kind_ref[k, odd] for k in members]
        for k, value in zip(members, extend([env_ref[k] for k in members], 0, kinds)):
            mid[k] = value

        @pl.when(is_odd)
        def _():
            for k in members:
                mid_copy(k).start()

        return carry

    @pl.when(is_odd)
    def _():
        set_basis(0, iso_ref, True)

        def turn(k, carry):
            rbuf[k] = env_ref[k].T
            return carry

        lax.fori_loop(0, terms, turn, 0)

    @pl.when(is_even)
    def _():
        set_basis(0, iso_ref, False)
        set_basis(2, iso_ref, True)

    count = 3 + jnp.where(is_even, 2, 0) + jnp.where(has_outward, 1, 0)
    pl.semaphore_wait(barrier, count)

    @pl.when(is_odd)
    def _():
        iso_copy.start()
        last_copy.start()

    @pl.when(is_even)
    def _():
        last_copy.start()
        env_copy.start()

    lax.fori_loop(0, terms // group, own_group, 0)

    @pl.when(is_even)
    def _():
        iso_copy.wait_recv()
        set_basis(1, piso, False)

        def fresh_group(i, carry):
            members = [group * i + m for m in range(group)]
            kinds = [kind_ref[k, 0] for k in members]
            for k, value in zip(members, extend([mid[k] for k in members], 1, kinds)):
                fresh[k] = value
                fresh_first(k).start()
            return carry

        lax.fori_loop(0, terms // group, fresh_group, 0)
        for g in range(1, PARTS):
            fresh_block(g).start()

        def right_group(i, carry):
            members = [group * i + m for m in range(group)]
            for k in members:
                mid_copy(k).wait_recv()
            kinds = [kind_ref[k, 1] for k in members]
            for k, value in zip(members, extend([came_mid[k] for k in members], 2, kinds)):
                rbuf[k] = value.T
            return carry

        lax.fori_loop(0, terms // group, right_group, 0)

    last_copy.wait_recv()
    for s in range(PHYS):
        for t in range(PHYS):
            value = matmul(came[s], first_ref[t])
            for part in range(PARTS):
                piece = value[part * rows : (part + 1) * rows]
                two_site[pairs * part + PHYS * s + t] = piece
                v[pairs * part + PHYS * s + t] = piece.astype(BF16)

    def right_of(n, g):
        lhs = jnp.concatenate([v[pairs * g + x] for x in range(pairs)], axis=0)
        for k in range(terms):
            value = matmul(lhs, rbuf[k]).astype(BF16)
            for x in range(pairs):
                h[n, k, x, block_of(g)] = value[x * rows : (x + 1) * rows]

    def first_right(g, carry):
        right_of(0, g)
        return carry

    lax.fori_loop(0, PARTS, first_right, 0)

    @pl.when(is_odd)
    def _():
        env_copy.wait_recv()

    def wait_block(g):
        @pl.when(g == 0)
        def _():
            for k in range(terms):
                fresh_first(k).wait_recv()

        @pl.when(g > 0)
        def _():
            fresh_block(g).wait_recv()

    def partial_of(n, g):
        if n == 0:

            @pl.when(is_even)
            def _():
                wait_block(g)

        for s in range(PHYS):
            for t in range(PHYS):
                total = None
                for k in range(terms):
                    kind_0, kind_1 = kind_ref[k, 0], kind_ref[k, 1]
                    flip_0, minus_0 = lax.rem(kind_0, 2), kind_0 // 2
                    flip_1, minus_1 = lax.rem(kind_1, 2), kind_1 // 2
                    from_s = flip_0 if s == 0 else 1 - flip_0
                    from_t = flip_1 if t == 0 else 1 - flip_1
                    sign = (1 - 2 * s * minus_0) * (1 - 2 * t * minus_1)
                    lhs = left[k, block_of(g)] * sign.astype(F32).astype(BF16)
                    value = matmul(lhs, h[n, k, PHYS * from_s + from_t])
                    total = value if total is None else total + value
                acc[n, pairs * g + PHYS * s + t] = total.astype(BF16)

    def pass_inward(n, j):
        @pl.when(has_outward)
        def _():
            arrived(n, 0, j).wait_recv()
            acc[n, j] = (acc[n, j].astype(F32) + recv[n, 0, j].astype(F32)).astype(BF16)

        in_copy(n, j).start()

    def pass_outward(n, j, squares):
        arrived(n, 1, j).wait_recv()
        came_in = recv[n, 1, j].astype(F32)
        own = jnp.where(middle, 1.0, 0.0)
        whole = (came_in + own * acc[n, j].astype(F32)).astype(BF16)

        @pl.when(has_outward)
        def _():
            tot[n, j] = whole
            out_copy(n, j).start()

        value = two_site[j] - step_size * whole.astype(F32)
        two_site[j] = value
        if n < STEPS - 1:
            v[j] = value.astype(BF16)
            return squares
        return squares + jnp.sum((value * value).reshape((rows // 8, 8, value.shape[1])), axis=0)

    lag = jnp.where(has_outward, min(LAG, chunks), chunks)
    zero = jnp.zeros((8, two_site.shape[2]), F32)
    for n in range(STEPS):

        def step(j, squares):
            @pl.when(jnp.logical_and(j < chunks, lax.rem(j, pairs) == 0))
            def _():
                partial_of(n, j // pairs)

            @pl.when(j < chunks)
            def _():
                pass_inward(n, j)

            return squares

        def body(j, squares):
            squares = step(j, squares)
            done = j - lag
            squares = pass_outward(n, done, squares)
            if n < STEPS - 1:

                @pl.when(lax.rem(done, pairs) == pairs - 1)
                def _():
                    right_of(n + 1, done // pairs)

            return squares

        lax.fori_loop(0, lag, step, 0)
        squares = lax.fori_loop(lag, chunks + lag, body, zero)

    size = two_site.shape[0] * two_site.shape[1] * two_site.shape[2]
    scale = lax.rsqrt(jnp.full((1, 1), jnp.sum(squares), F32) / size + epsilon)

    lanes = out_ref.shape[1]
    halves = two_site.shape[2] // lanes
    stride = pairs * halves
    for part in range(PARTS):
        for s in range(PHYS):
            for t in range(PHYS):
                for c in range(halves):
                    start = part * rows * stride + (s * halves + c) * PHYS + t
                    columns = pl.ds(c * lanes, lanes)
                    out_ref[pl.ds(start, rows, stride=stride), :] = (
                        two_site[pairs * part + PHYS * s + t, :, columns] * scale
                    )

    last_copy.wait_send()

    @pl.when(is_odd)
    def _():
        iso_copy.wait_send()

        def drain_mid(k, carry):
            mid_copy(k).wait_send()
            return carry

        lax.fori_loop(0, terms, drain_mid, 0)

    @pl.when(is_even)
    def _():
        env_copy.wait_send()

        def drain_fresh(k, carry):
            fresh_first(k).wait_send()
            return carry

        lax.fori_loop(0, terms, drain_fresh, 0)
        for g in range(1, PARTS):
            fresh_block(g).wait_send()

    for n in range(STEPS):

        def drain_chunk(x, carry):
            in_copy(n, x).wait_send()

            @pl.when(has_outward)
            def _():
                out_copy(n, x).wait_send()

            return carry

        lax.fori_loop(0, chunks, drain_chunk, 0)


def shards(n_sec, n_term, meet_env, meet_iso, last_site, first_site, term_kind):
    terms, bond = meet_env.shape[1], meet_env.shape[2]
    pairs = PHYS * PHYS

    def by_level(site):
        return jnp.transpose(site[0], (1, 0, 2))

    vmem = pl.BlockSpec(memory_space=pltpu.VMEM)
    block = (bond, bond)
    chunks = pairs * PARTS
    strip = (bond // PARTS, bond)
    lanes = min(bond, 128)
    dma = pltpu.SemaphoreType.DMA
    out = pl.pallas_call(
        functools.partial(kernel, n_sec, n_term, terms),
        out_shape=jax.ShapeDtypeStruct((pairs * bond * bond // lanes, lanes), F32),
        in_specs=[pl.BlockSpec(memory_space=pltpu.SMEM)] + [vmem] * 4,
        out_specs=vmem,
        scratch_shapes=[
            pltpu.VMEM((terms,) + block, BF16),
            pltpu.VMEM((terms,) + block, BF16),
            pltpu.VMEM((terms,) + block, BF16),
            pltpu.VMEM((terms,) + block, BF16),
            pltpu.VMEM((terms,) + block, BF16),
            pltpu.VMEM((PHYS,) + block, BF16),
            pltpu.VMEM((PHYS,) + block, BF16),
            pltpu.VMEM((3, PHYS) + block, BF16),
            pltpu.VMEM((3, 3) + block, BF16),
            pltpu.VMEM((STEPS, terms, pairs) + block, BF16),
            pltpu.VMEM((chunks,) + strip, BF16),
            pltpu.VMEM((chunks,) + strip, F32),
            pltpu.VMEM((STEPS, chunks) + strip, BF16),
            pltpu.VMEM((STEPS, chunks) + strip, BF16),
            pltpu.VMEM((STEPS, 2, chunks) + strip, BF16),
            dma((3,)),
            dma((3,)),
            dma((terms,)),
            dma((terms,)),
            dma((terms + PARTS - 1,)),
            dma((terms + PARTS - 1,)),
            dma((STEPS, chunks)),
            dma((STEPS, 2, chunks)),
            dma((STEPS, chunks)),
        ],
        compiler_params=pltpu.CompilerParams(
            collective_id=0, has_side_effects=True, vmem_limit_bytes=48 * 1024 * 1024
        ),
    )(term_kind, meet_env[0], by_level(meet_iso), by_level(last_site), by_level(first_site))
    out = out.reshape(bond, PHYS, bond // lanes, PHYS, lanes)
    out = jnp.transpose(out, (0, 1, 3, 2, 4))
    return out.reshape(1, bond, PHYS, PHYS, bond)


def solution(mesh):
    in_specs = (
        P("sec", "term", None, None),
        P("sec", None, None, None),
        P("sec", None, None, None),
        P("sec", None, None, None),
        P("term", None),
    )
    out_specs = P("sec", None, None, None, None)
    body = functools.partial(shards, mesh.shape["sec"], mesh.shape["term"])
    return jax.shard_map(body, mesh=mesh, in_specs=in_specs, out_specs=out_specs, check_vma=False)
```

time: 54.1 us -> 50.7 us (0.937)
  Pallas kernels: 50.9 us -> 47.6 us
    pallas_call x1, Pallas kernels: 50.9 us -> 47.6 us  [shards(): pl.pallas_call(functools.partial(kernel, n_sec, n_term, terms), out_shape...]
where the time goes in v1:
time: 50.7 us; the launch traced here: 50.6 us
  Pallas kernels  47.6 us (94%)
  local copies, waits for them, and re-layouts  2.97 us (6%)
    pallas_call x1, Pallas kernels, shards(): pl.pallas_call(functools.partial(kernel, n_sec, n_term, terms), out_shape...  47.6 us
    unnamed x11, local copies, waits for them, and re-layouts  2.89 us

profile of v1, /device:TPU:0, one launch (start us, length us, event | category | flops | bytes accessed | tf_op | source)
XLA Modules:
  0.0 50.6 jit_solution(13466150229146720754)
XLA Ops:
  0.0 0.0 copy-start.3
  0.0 0.0 copy-start.1
  0.0 0.0 copy-start.2
  0.0 0.7 %copy-done.3 = s32[6,2]{0,1:T(2,128)S(1)} copy-done((s32[6,2]{0,1:T(2,128)S(1)}, s32[6,2]{0,1:T(2,128)}, u32[]{:S(2)}) %copy-start.3) | copy-done | bytes 72
  0.7 0.1 copy.9.kind_ref
  0.8 0.0 copy-start
  0.8 1.1 %copy.14 = bf16[1,256,2,256]{3,1,2,0:T(8,128)(2,1)S(1)} copy(bf16[1,256,2,256]{3,2,1,0:T(2,128)(2,1)} %param.6) | data formatting | bytes 524288 | tf_op args[1]
  1.8 0.0 copy-done.1
  1.8 0.0 copy-done.2
  1.8 0.1 copy_bitcast_fusion
  1.9 0.1 copy-done
  2.0 47.6 %shard_map.55 = f32[2048,128]{1,0:T(8,128)S(1)} custom-call(s32[6,2]{1,0:T(8,128)S(1)} %copy.9.kind_ref, bf16[6,256,256]{2,1,0:T(8,128)(2,1)S(1)} %bitcast.21, bf16[2,256,256]{2,1,0:T(8,128)(2,1)S(1)} %bitcast.20, bf16[2,256,256]{2,1,0:T(8,128)(2,1)S(1)} %get-tuple-element.6.last_ref, bf16[2,256,256]{2,1,0:T(8,128)(2,1)S(1)} %get-tuple-element.5.first_ref), custom_call_target="tpu_custom_call" | custom-call | tf_op jit(solution)/shard_map/pallas_call | solution.py:442
  49.6 1.0 %copy.16 = f32[1,256,2,2,256]{4,3,2,1,0:T(2,128)} copy(f32[1,256,2,2,256]{4,3,2,1,0:T(2,128)S(1)} %bitcast.19) | data formatting | bytes 2097152
Async XLA Ops:
  0.0 0.7 %copy-start.3 = (s32[6,2]{0,1:T(2,128)S(1)}, s32[6,2]{0,1:T(2,128)}, u32[]{:S(2)}) copy-start(s32[6,2]{0,1:T(2,128)} %param.9) | copy-start | bytes 148
  0.0 1.8 %copy-start.1 = (bf16[1,256,2,256]{3,2,1,0:T(2,128)(2,1)S(1)}, bf16[1,256,2,256]{3,2,1,0:T(2,128)(2,1)}, u32[]{:S(2)}) copy-start(bf16[1,256,2,256]{3,2,1,0:T(2,128)(2,1)} %param.8) | copy-start | bytes 786436
  0.0 1.8 %copy-start.2 = (bf16[1,256,2,256]{3,2,1,0:T(2,128)(2,1)S(1)}, bf16[1,256,2,256]{3,2,1,0:T(2,128)(2,1)}, u32[]{:S(2)}) copy-start(bf16[1,256,2,256]{3,2,1,0:T(2,128)(2,1)} %param.7) | copy-start | bytes 786436
  0.8 1.3 %copy-start = (bf16[1,6,256,256]{3,2,1,0:T(8,128)(2,1)S(1)}, bf16[1,6,256,256]{3,2,1,0:T(8,128)(2,1)}, u32[]{:S(2)}) copy-start(bf16[1,6,256,256]{3,2,1,0:T(8,128)(2,1)} %param.5) | copy-start | bytes 2359300

commit v2 on v1

v2 whole, which is shorter than its diff:
```python
import functools

import jax
import jax.numpy as jnp
from jax import lax
from jax.experimental import pallas as pl
from jax.experimental.pallas import tpu as pltpu
from jax.sharding import PartitionSpec as P

PHYS = 2
STEPS = 2
PARTS = 4
LAG = 8
GROUP = 2
step_size = 0.2
epsilon = 1e-06
F32 = jnp.float32
BF16 = jnp.bfloat16
MESH = pl.DeviceIdType.MESH


def matmul(lhs, rhs):
    return jnp.dot(lhs, rhs, preferred_element_type=F32)


def kernel(
    n_sec,
    n_term,
    terms,
    kind_hbm,
    env_hbm,
    iso_hbm,
    last_hbm,
    first_hbm,
    out_ref,
    kind_ref,
    env_ref,
    raw,
    sites,
    left,
    rbuf,
    mid,
    came_env,
    fresh,
    piso,
    came,
    basis,
    table,
    h,
    v,
    two_site,
    acc,
    tot,
    recv,
    load,
    one_send,
    one_recv,
    last_send,
    last_recv,
    fresh_send,
    fresh_recv,
    in_send,
    chunk_recv,
    out_send,
):
    pairs = PHYS * PHYS
    rows = left.shape[1] // PARTS
    chunks = pairs * PARTS
    sec = lax.axis_index("sec")
    term = lax.axis_index("term")
    odd = lax.rem(sec, 2)
    is_odd = odd == 1
    is_even = odd == 0
    partner = sec + 1 - 2 * odd
    following = lax.rem(sec + 1, n_sec)
    before = lax.rem(sec + n_sec - 1, n_sec)
    ahead = lax.rem(sec + 2, n_sec)
    behind = lax.rem(sec + n_sec - 2, n_sec)
    half = n_term // 2
    left_side = term < half
    inward = jnp.where(left_side, term + 1, term - 1)
    outward = jnp.where(left_side, term - 1, term + 1)
    has_outward = jnp.logical_and(term > 0, term < n_term - 1)
    middle = jnp.logical_or(term == half - 1, term == half)
    in_slot = jnp.where(middle, 1, 0)
    is_end = jnp.logical_not(has_outward)
    own_level = lax.rem(term, 2)
    beside = term + 1 - 2 * own_level
    iso_ref, last_ref, first_ref = sites.at[0], sites.at[1], sites.at[2]

    def at(s, t):
        return dict(device_id=(s, t), device_id_type=MESH)

    barrier = pltpu.get_barrier_semaphore()
    pl.semaphore_signal(barrier, inc=1, **at(partner, term))
    pl.semaphore_signal(barrier, inc=1, **at(sec, inward))

    @pl.when(has_outward)
    def _():
        pl.semaphore_signal(barrier, inc=1, **at(sec, outward))

    @pl.when(is_even)
    def _():
        for s in (behind, before):
            pl.semaphore_signal(barrier, inc=1, **at(s, term))

    loads = [
        pltpu.make_async_copy(src, dst, load.at[i])
        for i, (src, dst) in enumerate(
            (
                (iso_hbm, raw.at[0]),
                (last_hbm, raw.at[1]),
                (first_hbm, raw.at[2]),
                (kind_hbm, kind_ref),
                (env_hbm, env_ref),
            )
        )
    ]
    for i in (0, 1, 4, 3, 2):
        loads[i].start()

    def remote(src, dst, send, receive, s, t):
        return pltpu.make_async_remote_copy(
            src_ref=src, dst_ref=dst, send_sem=send, recv_sem=receive, **at(s, t)
        )

    iso_copy = remote(iso_ref, piso, one_send.at[0], one_recv.at[0], partner, term)
    env_copy = remote(env_ref, left, one_send.at[1], one_recv.at[1], partner, term)
    side_copy = remote(env_ref, came_env, one_send.at[1], one_recv.at[1], partner, term)

    def last_copy(level):
        return remote(
            last_ref.at[level],
            came.at[level],
            last_send.at[level],
            last_recv.at[level],
            following,
            term,
        )

    def share_copy(level):
        return remote(
            came.at[level], came.at[level], one_send.at[2], last_recv.at[level], sec, beside
        )


    def block_of(g):
        return pl.ds(pl.multiple_of(g * rows, rows), rows)

    def fresh_first(k):
        return remote(
            fresh.at[k, pl.ds(0, rows)],
            left.at[k, pl.ds(0, rows)],
            fresh_send.at[0],
            fresh_recv.at[0],
            ahead,
            term,
        )

    def fresh_block(g):
        return remote(
            fresh.at[:, block_of(g)],
            left.at[:, block_of(g)],
            fresh_send.at[0],
            fresh_recv.at[g],
            ahead,
            term,
        )

    def recv_row(n, slot):
        return slot * (1 + n)

    def in_copy(n, x):
        return remote(
            acc.at[n, x],
            recv.at[n, in_slot, x],
            in_send.at[n],
            chunk_recv.at[recv_row(n, in_slot), x],
            sec,
            inward,
        )

    def out_copy(n, x):
        return remote(
            tot.at[n, x],
            recv.at[n, 1, x],
            out_send.at[n],
            chunk_recv.at[recv_row(n, 1), x],
            sec,
            outward,
        )

    def arrived(n, slot, x):
        return remote(
            acc.at[n, x],
            recv.at[n, slot, x],
            in_send.at[n],
            chunk_recv.at[recv_row(n, slot), x],
            sec,
            inward,
        )

    def set_basis(which, source, flip):
        for s in range(PHYS):
            value = source[s]
            turned = value.T
            basis[which, s] = turned if flip else value
            table[which, s] = value if flip else turned
            if s == 1:
                table[which, 2] = -value if flip else -turned

    def extend(values, which, kinds):
        wide = [
            [matmul(value, basis[which, r]).astype(BF16) for r in range(PHYS)] for value in values
        ]
        results = []
        for (wide_0, wide_1), kind in zip(wide, kinds):
            first = jnp.where(kind == 1, 1, jnp.where(kind == 3, 2, 0))
            second = jnp.where(kind == 0, 1, jnp.where(kind == 2, 2, 0))
            result = matmul(table[which, first], wide_0) + matmul(table[which, second], wide_1)
            results.append(result.astype(BF16))
        return results

    group = GROUP if terms % GROUP == 0 else 1

    def own_group(i, carry):
        members = [group * i + m for m in range(group)]
        kinds = [kind_ref[0, k] for k in members]
        for k, value in zip(members, extend([env_ref[k] for k in members], 0, kinds)):
            mid[k] = value
        return carry

    def split_levels(i):
        sites[i] = jnp.transpose(raw[i], (1, 0, 2))

    loads[0].wait()
    split_levels(0)
    loads[1].wait()
    split_levels(1)
    loads[4].wait()
    loads[3].wait()

    @pl.when(is_odd)
    def _():
        def turn(k, carry):
            rbuf[k] = env_ref[k].T
            return carry

        lax.fori_loop(0, terms, turn, 0)

    @pl.when(is_even)
    def _():
        set_basis(0, iso_ref, False)
        own_group(0, 0)

    pl.semaphore_wait(barrier, 3 + jnp.where(has_outward, 1, 0))

    @pl.when(is_odd)
    def _():
        iso_copy.start()
        last_copy(own_level).start()
        side_copy.start()
        loads[2].wait()
        split_levels(2)

    @pl.when(is_even)
    def _():
        for s in range(PHYS):
            last_copy(s).start()
        env_copy.start()
        lax.fori_loop(1, terms // group, own_group, 0)

    @pl.when(is_even)
    def _():
        iso_copy.wait_recv()
        set_basis(1, piso, False)

        def fresh_group(i, carry):
            members = [group * i + m for m in range(group)]
            kinds = [kind_ref[0, k] for k in members]
            for k, value in zip(members, extend([mid[k] for k in members], 1, kinds)):
                fresh[k] = value
                fresh_first(k).start()
            return carry

        lax.fori_loop(0, terms // group, fresh_group, 0)
        for g in range(1, PARTS):
            fresh_block(g).start()

        def right_group(i, carry):
            members = [group * i + m for m in range(group)]
            kinds = [kind_ref[1, k] for k in members]
            for k, value in zip(members, extend(extend([came_env[k] for k in members], 3, kinds), 2, kinds)):
                rbuf[k] = value.T

            @pl.when(i == 0)
            def _():
                last_copy(own_level).wait_recv()
                share_copy(own_level).start()

            return carry

        set_basis(2, iso_ref, True)
        set_basis(3, piso, True)
        loads[2].wait()
        split_levels(2)
        side_copy.wait_recv()
        lax.fori_loop(0, terms // group, right_group, 0)

    def first_right(i, carry):
        level = jnp.where(is_even, own_level + i - 2 * own_level * i, i)

        @pl.when(jnp.logical_or(is_odd, i > 0))
        def _():
            last_copy(level).wait_recv()

        for t in range(PHYS):
            x = PHYS * level + t
            value = matmul(came[level], first_ref[t])
            rounded = value.astype(BF16)
            for part in range(PARTS):
                two_site[pairs * part + x] = value[part * rows : (part + 1) * rows]
                v[pairs * part + x] = rounded[part * rows : (part + 1) * rows]
            for k in range(terms):
                h[0, k, x] = matmul(rounded, rbuf[k]).astype(BF16)
        return carry

    lax.fori_loop(0, PHYS, first_right, 0)

    def right_of(n, g):
        lhs = jnp.concatenate([v[pairs * g + x] for x in range(pairs)], axis=0)
        for k in range(terms):
            value = matmul(lhs, rbuf[k]).astype(BF16)
            for x in range(pairs):
                h[n, k, x, block_of(g)] = value[x * rows : (x + 1) * rows]

    @pl.when(is_odd)
    def _():
        env_copy.wait_recv()

    def wait_block(g):
        fresh_block(g).wait_recv()

    def chunk_sum(n, g, s, t):
        total = None
        for k in range(terms):
            kind_0, kind_1 = kind_ref[0, k], kind_ref[1, k]
            flip_0, minus_0 = lax.rem(kind_0, 2), kind_0 // 2
            flip_1, minus_1 = lax.rem(kind_1, 2), kind_1 // 2
            from_s = s + flip_0 - 2 * s * flip_0
            from_t = t + flip_1 - 2 * t * flip_1
            sign = (1 - 2 * s * minus_0) * (1 - 2 * t * minus_1)
            lhs = left[k, block_of(g)] * sign.astype(F32).astype(BF16)
            value = matmul(lhs, h[n, k, PHYS * from_s + from_t])
            total = value if total is None else total + value
        return total.astype(BF16)

    def partial_of(n, g):
        if n == 0:

            @pl.when(is_even)
            def _():
                wait_block(g)

        for s in range(PHYS):
            for t in range(PHYS):
                acc[n, pairs * g + PHYS * s + t] = chunk_sum(n, g, s, t)

    def send_partial(n, j):
        x = lax.rem(j, pairs)
        if n == 0:

            @pl.when(jnp.logical_and(is_even, x == 0))
            def _():
                wait_block(j // pairs)

        acc[n, j] = chunk_sum(n, j // pairs, x // PHYS, lax.rem(x, PHYS))
        in_copy(n, j).start()

    def pass_inward(n, j):
        arrived(n, 0, j).wait_recv()
        acc[n, j] = (acc[n, j].astype(F32) + recv[n, 0, j].astype(F32)).astype(BF16)
        in_copy(n, j).start()

    def pass_outward(n, j, squares):
        arrived(n, 1, j).wait_recv()
        came_in = recv[n, 1, j].astype(F32)
        own = jnp.where(middle, 1.0, 0.0)
        whole = (came_in + own * acc[n, j].astype(F32)).astype(BF16)

        @pl.when(has_outward)
        def _():
            tot[n, j] = whole
            out_copy(n, j).start()

        value = two_site[j] - step_size * whole.astype(F32)
        two_site[j] = value
        if n < STEPS - 1:
            v[j] = value.astype(BF16)
            return squares
        return squares + jnp.sum((value * value).reshape((rows // 8, 8, value.shape[1])), axis=0)

    lag = jnp.where(has_outward, min(LAG, chunks), chunks)
    begin = jnp.where(has_outward, 0, chunks)
    zero = jnp.zeros((8, two_site.shape[2]), F32)
    for n in range(STEPS):
        gated = jnp.logical_and(is_even, has_outward) if n == 0 else False
        ready = jnp.where(jnp.logical_or(gated, is_end), 0, PARTS)
        sending = jnp.where(is_end, chunks, 0)

        def ahead_of(g, carry):
            partial_of(n, g)
            return carry

        def sent(j, carry):
            send_partial(n, j)
            return carry

        def step(j, squares):
            @pl.when(j < chunks)
            def _():
                if n == 0:

                    @pl.when(jnp.logical_and(gated, lax.rem(j, pairs) == 0))
                    def _():
                        partial_of(n, j // pairs)

                pass_inward(n, j)

            return squares

        def body(j, squares):
            squares = step(j, squares)
            done = j - lag
            squares = pass_outward(n, done, squares)
            if n < STEPS - 1:

                @pl.when(lax.rem(done, pairs) == pairs - 1)
                def _():
                    right_of(n + 1, done // pairs)

            return squares

        lax.fori_loop(0, ready, ahead_of, 0)
        lax.fori_loop(0, sending, sent, 0)
        lax.fori_loop(begin, lag, step, 0)
        squares = lax.fori_loop(lag, chunks + lag, body, zero)

    size = two_site.shape[0] * two_site.shape[1] * two_site.shape[2]
    scale = lax.rsqrt(jnp.full((1, 1), jnp.sum(squares), F32) / size + epsilon)

    lanes = out_ref.shape[1]
    halves = two_site.shape[2] // lanes
    stride = pairs * halves
    for part in range(PARTS):
        for s in range(PHYS):
            for t in range(PHYS):
                for c in range(halves):
                    start = part * rows * stride + (s * halves + c) * PHYS + t
                    columns = pl.ds(c * lanes, lanes)
                    out_ref[pl.ds(start, rows, stride=stride), :] = (
                        two_site[pairs * part + PHYS * s + t, :, columns] * scale
                    )


    @pl.when(is_odd)
    def _():
        iso_copy.wait_send()
        last_copy(own_level).wait_send()
        side_copy.wait_send()

    @pl.when(is_even)
    def _():
        for s in range(PHYS):
            last_copy(s).wait_send()
        env_copy.wait_send()
        share_copy(own_level).wait_send()

        remote(fresh, left, fresh_send.at[0], fresh_recv.at[0], ahead, term).wait_send()

    for n in range(STEPS):
        remote(
            acc.at[n], recv.at[n, 0], in_send.at[n], chunk_recv.at[0, 0], sec, inward
        ).wait_send()

        @pl.when(has_outward)
        def _():
            remote(
                tot.at[n], recv.at[n, 0], out_send.at[n], chunk_recv.at[0, 0], sec, outward
            ).wait_send()


def shards(n_sec, n_term, meet_env, meet_iso, last_site, first_site, term_kind):
    terms, bond = meet_env.shape[1], meet_env.shape[2]
    pairs = PHYS * PHYS

    vmem = pl.BlockSpec(memory_space=pltpu.VMEM)
    block = (bond, bond)
    chunks = pairs * PARTS
    strip = (bond // PARTS, bond)
    lanes = min(bond, 128)
    dma = pltpu.SemaphoreType.DMA
    out = pl.pallas_call(
        functools.partial(kernel, n_sec, n_term, terms),
        out_shape=jax.ShapeDtypeStruct((pairs * bond * bond // lanes, lanes), F32),
        in_specs=[pl.BlockSpec(memory_space=pltpu.HBM)] * 5,
        out_specs=vmem,
        scratch_shapes=[
            pltpu.SMEM(term_kind.shape[::-1], jnp.int32),
            pltpu.VMEM((terms,) + block, BF16),
            pltpu.VMEM((3, bond, PHYS, bond), BF16),
            pltpu.VMEM((3, PHYS) + block, BF16),
            pltpu.VMEM((terms,) + block, BF16),
            pltpu.VMEM((terms,) + block, BF16),
            pltpu.VMEM((terms,) + block, BF16),
            pltpu.VMEM((terms,) + block, BF16),
            pltpu.VMEM((terms,) + block, BF16),
            pltpu.VMEM((PHYS,) + block, BF16),
            pltpu.VMEM((PHYS,) + block, BF16),
            pltpu.VMEM((4, PHYS) + block, BF16),
            pltpu.VMEM((4, 3) + block, BF16),
            pltpu.VMEM((STEPS, terms, pairs) + block, BF16),
            pltpu.VMEM((chunks,) + strip, BF16),
            pltpu.VMEM((chunks,) + strip, F32),
            pltpu.VMEM((STEPS, chunks) + strip, BF16),
            pltpu.VMEM((STEPS, chunks) + strip, BF16),
            pltpu.VMEM((STEPS, 2, chunks) + strip, BF16),
            dma((5,)),
            dma((3,)),
            dma((2,)),
            dma((PHYS,)),
            dma((PHYS,)),
            dma((1,)),
            dma((PARTS,)),
            dma((STEPS,)),
            dma((1 + STEPS, chunks)),
            dma((STEPS,)),
        ],
        compiler_params=pltpu.CompilerParams(
            collective_id=0, has_side_effects=True, vmem_limit_bytes=48 * 1024 * 1024
        ),
    )(*(pltpu.with_memory_space_constraint(a, pltpu.HBM) for a in (term_kind.T, meet_env[0], meet_iso[0], last_site[0], first_site[0])))
    out = out.reshape(bond, PHYS, bond // lanes, PHYS, lanes)
    out = jnp.transpose(out, (0, 1, 3, 2, 4))
    return out.reshape(1, bond, PHYS, PHYS, bond)


def solution(mesh):
    in_specs = (
        P("sec", "term", None, None),
        P("sec", None, None, None),
        P("sec", None, None, None),
        P("sec", None, None, None),
        P("term", None),
    )
    out_specs = P("sec", None, None, None, None)
    body = functools.partial(shards, mesh.shape["sec"], mesh.shape["term"])
    return jax.shard_map(body, mesh=mesh, in_specs=in_specs, out_specs=out_specs, check_vma=False)
```

time: 50.7 us -> 46.4 us (0.915)
  Pallas kernels: 47.6 us -> 45.3 us
  local copies, waits for them, and re-layouts: 2.97 us -> 0.97 us
    pallas_call x1, Pallas kernels: 47.6 us -> 45.3 us  [shards(): pl.pallas_call(functools.partial(kernel, n_sec, n_term, terms), out_shape...]
    unnamed x11 -> x1, local copies, waits for them, and re-layouts: 2.89 us -> 0.97 us
where the time goes in v2:
time: 46.4 us; the launch traced here: 46.3 us
  Pallas kernels  45.3 us (98%)
  local copies, waits for them, and re-layouts  0.97 us (2%)
    pallas_call x1, Pallas kernels, shards(): pl.pallas_call(functools.partial(kernel, n_sec, n_term, terms), out_shape...  45.3 us
    unnamed x1, local copies, waits for them, and re-layouts  0.97 us

profile of v2, /device:TPU:0, one launch (start us, length us, event | category | flops | bytes accessed | tf_op | source)
XLA Modules:
  0.0 46.3 jit_solution(3829578458248233052)
XLA Ops:
  0.0 45.3 %shard_map.55 = f32[2048,128]{1,0:T(8,128)S(1)} custom-call(s32[2,6]{1,0:T(2,128)} %bitcast.15, bf16[6,256,256]{2,1,0:T(8,128)(2,1)} %bitcast.11, bf16[256,2,256]{2,1,0:T(2,128)(2,1)} %bitcast.12, bf16[256,2,256]{2,1,0:T(2,128)(2,1)} %bitcast.13, bf16[256,2,256]{2,1,0:T(2,128)(2,1)} %bitcast.14), custom_call_target="tpu_custom_call" | custom-call | tf_op jit(solution)/shard_map/pallas_call | solution.py:503
  45.3 1.0 %copy.8 = f32[1,256,2,2,256]{4,3,2,1,0:T(2,128)} copy(f32[1,256,2,2,256]{4,3,2,1,0:T(2,128)S(1)} %bitcast.10) | data formatting | bytes 2097152

commit v3 on v2

--- a/solution.py
+++ b/solution.py
@@ -11,7 +11,8 @@
 STEPS = 2
 PARTS = 4
 LAG = 8
-GROUP = 2
+GROUP = 6
+SIDE = 6
 step_size = 0.2
 epsilon = 1e-06
 F32 = jnp.float32
@@ -128,21 +129,33 @@
     env_copy = remote(env_ref, left, one_send.at[1], one_recv.at[1], partner, term)
     side_copy = remote(env_ref, came_env, one_send.at[1], one_recv.at[1], partner, term)
 
-    def last_copy(level):
-        return remote(
-            last_ref.at[level],
-            came.at[level],
-            last_send.at[level],
-            last_recv.at[level],
+    last_whole = remote(last_ref, came, last_send.at[0], last_recv.at[0], partner, term)
+    kept = left.shape[1] - rows
+
+    def half_of(site, level, upper):
+        return site.at[level, pl.ds(kept, rows) if upper else pl.ds(0, kept)]
+
+    last_parts = [
+        remote(
+            half_of(last_ref, level, upper),
+            half_of(came, level, upper),
+            last_send.at[i],
+            last_recv.at[i],
             following,
             term,
         )
-
-    def share_copy(level):
-        return remote(
-            came.at[level], came.at[level], one_send.at[2], last_recv.at[level], sec, beside
-        )
-
+        for i, (level, upper) in enumerate(
+            ((own_level, True), (own_level, False), (1 - own_level, False))
+        )
+    ]
+    share_copy = remote(
+        half_of(came, own_level, True),
+        half_of(came, own_level, True),
+        one_send.at[2],
+        last_recv.at[3],
+        sec,
+        beside,
+    )
 
     def block_of(g):
         return pl.ds(pl.multiple_of(g * rows, rows), rows)
@@ -222,6 +235,7 @@
         return results
 
     group = GROUP if terms % GROUP == 0 else 1
+    side_group = SIDE if terms % SIDE == 0 else 1
 
     def own_group(i, carry):
         members = [group * i + m for m in range(group)]
@@ -237,11 +251,25 @@
     split_levels(0)
     loads[1].wait()
     split_levels(1)
+
+    pl.semaphore_wait(barrier, 3 + jnp.where(has_outward, 1, 0))
+
+    @pl.when(is_odd)
+    def _():
+        iso_copy.start()
+        for copy in last_parts:
+            copy.start()
+
+    @pl.when(is_even)
+    def _():
+        last_whole.start()
+
     loads[4].wait()
-    loads[3].wait()
 
     @pl.when(is_odd)
     def _():
+        side_copy.start()
+
         def turn(k, carry):
             rbuf[k] = env_ref[k].T
             return carry
@@ -250,25 +278,19 @@
 
     @pl.when(is_even)
     def _():
+        env_copy.start()
+
+    loads[3].wait()
+
+    @pl.when(is_even)
+    def _():
         set_basis(0, iso_ref, False)
-        own_group(0, 0)
-
-    pl.semaphore_wait(barrier, 3 + jnp.where(has_outward, 1, 0))
+        lax.fori_loop(0, terms // group, own_group, 0)
 
     @pl.when(is_odd)
     def _():
-        iso_copy.start()
-        last_copy(own_level).start()
-        side_copy.start()
         loads[2].wait()
         split_levels(2)
-
-    @pl.when(is_even)
-    def _():
-        for s in range(PHYS):
-            last_copy(s).start()
-        env_copy.start()
-        lax.fori_loop(1, terms // group, own_group, 0)
 
     @pl.when(is_even)
     def _():
@@ -288,15 +310,15 @@
             fresh_block(g).start()
 
         def right_group(i, carry):
-            members = [group * i + m for m in range(group)]
+            members = [side_group * i + m for m in range(side_group)]
             kinds = [kind_ref[1, k] for k in members]
             for k, value in zip(members, extend(extend([came_env[k] for k in members], 3, kinds), 2, kinds)):
                 rbuf[k] = value.T
 
             @pl.when(i == 0)
             def _():
-                last_copy(own_level).wait_recv()
-                share_copy(own_level).start()
+                last_parts[0].wait_recv()
+                share_copy.start()
 
             return carry
 
@@ -305,14 +327,30 @@
         loads[2].wait()
         split_levels(2)
         side_copy.wait_recv()
-        lax.fori_loop(0, terms // group, right_group, 0)
+        lax.fori_loop(0, terms // side_group, right_group, 0)
 
     def first_right(i, carry):
         level = jnp.where(is_even, own_level + i - 2 * own_level * i, i)
 
-        @pl.when(jnp.logical_or(is_odd, i > 0))
+        @pl.when(jnp.logical_and(is_odd, i == 0))
         def _():
-            last_copy(level).wait_recv()
+            last_whole.wait_recv()
+
+        @pl.when(jnp.logical_and(is_even, i == 0))
+        def _():
+            last_parts[1].wait_recv()
+
+        @pl.when(jnp.logical_and(is_even, i > 0))
+        def _():
+            last_parts[2].wait_recv()
+            remote(
+                half_of(came, 1 - own_level, True),
+                half_of(came, 1 - own_level, True),
+                one_send.at[2],
+                last_recv.at[3],
+                sec,
+                beside,
+            ).wait_recv()
 
         for t in range(PHYS):
             x = PHYS * level + t
@@ -377,6 +415,10 @@
         acc[n, j] = chunk_sum(n, j // pairs, x // PHYS, lax.rem(x, PHYS))
         in_copy(n, j).start()
 
+    lanes = out_ref.shape[1]
+    halves = two_site.shape[2] // lanes
+    stride = pairs * halves
+
     def pass_inward(n, j):
         arrived(n, 0, j).wait_recv()
         acc[n, j] = (acc[n, j].astype(F32) + recv[n, 0, j].astype(F32)).astype(BF16)
@@ -394,10 +436,16 @@
             out_copy(n, j).start()
 
         value = two_site[j] - step_size * whole.astype(F32)
-        two_site[j] = value
         if n < STEPS - 1:
+            two_site[j] = value
             v[j] = value.astype(BF16)
             return squares
+        x = lax.rem(j, pairs)
+        start = (j // pairs) * (rows * stride) + (x // PHYS) * (halves * PHYS) + lax.rem(x, PHYS)
+        for c in range(halves):
+            out_ref[pl.ds(start + c * PHYS, rows, stride=stride), :] = value[
+                :, c * lanes : (c + 1) * lanes
+            ]
         return squares + jnp.sum((value * value).reshape((rows // 8, 8, value.shape[1])), axis=0)
 
     lag = jnp.where(has_outward, min(LAG, chunks), chunks)
@@ -405,7 +453,7 @@
     zero = jnp.zeros((8, two_site.shape[2]), F32)
     for n in range(STEPS):
         gated = jnp.logical_and(is_even, has_outward) if n == 0 else False
-        ready = jnp.where(jnp.logical_or(gated, is_end), 0, PARTS)
+        ready = jnp.where(is_end, 0, jnp.where(gated, 1, PARTS))
         sending = jnp.where(is_end, chunks, 0)
 
         def ahead_of(g, carry):
@@ -421,9 +469,13 @@
             def _():
                 if n == 0:
 
-                    @pl.when(jnp.logical_and(gated, lax.rem(j, pairs) == 0))
+                    @pl.when(
+                        jnp.logical_and(
+                            gated, jnp.logical_and(lax.rem(j, pairs) == 0, j < chunks - pairs)
+                        )
+                    )
                     def _():
-                        partial_of(n, j // pairs)
+                        partial_of(n, j // pairs + 1)
 
                 pass_inward(n, j)
 
@@ -449,32 +501,21 @@
     size = two_site.shape[0] * two_site.shape[1] * two_site.shape[2]
     scale = lax.rsqrt(jnp.full((1, 1), jnp.sum(squares), F32) / size + epsilon)
 
-    lanes = out_ref.shape[1]
-    halves = two_site.shape[2] // lanes
-    stride = pairs * halves
-    for part in range(PARTS):
-        for s in range(PHYS):
-            for t in range(PHYS):
-                for c in range(halves):
-                    start = part * rows * stride + (s * halves + c) * PHYS + t
-                    columns = pl.ds(c * lanes, lanes)
-                    out_ref[pl.ds(start, rows, stride=stride), :] = (
-                        two_site[pairs * part + PHYS * s + t, :, columns] * scale
-                    )
+    out_ref[...] = out_ref[...] * scale
 
 
     @pl.when(is_odd)
     def _():
         iso_copy.wait_send()
-        last_copy(own_level).wait_send()
+        for copy in last_parts:
+            copy.wait_send()
         side_copy.wait_send()
 
     @pl.when(is_even)
     def _():
-        for s in range(PHYS):
-            last_copy(s).wait_send()
+        last_whole.wait_send()
         env_copy.wait_send()
-        share_copy(own_level).wait_send()
+        share_copy.wait_send()
 
         remote(fresh, left, fresh_send.at[0], fresh_recv.at[0], ahead, term).wait_send()
 
@@ -528,8 +569,8 @@
             dma((5,)),
             dma((3,)),
             dma((2,)),
-            dma((PHYS,)),
-            dma((PHYS,)),
+            dma((3,)),
+            dma((4,)),
             dma((1,)),
             dma((PARTS,)),
             dma((STEPS,)),

time: 46.4 us -> 45.3 us (0.976)
  Pallas kernels: 45.3 us -> 44.2 us
    pallas_call x1, Pallas kernels: 45.3 us -> 44.2 us  [shards(): pl.pallas_call(functools.partial(kernel, n_sec, n_term, terms), out_shape...]
where the time goes in v3:
time: 45.3 us; the launch traced here: 45.2 us
  Pallas kernels  44.2 us (98%)
  local copies, waits for them, and re-layouts  0.97 us (2%)
    pallas_call x1, Pallas kernels, shards(): pl.pallas_call(functools.partial(kernel, n_sec, n_term, terms), out_shape...  44.2 us
    unnamed x1, local copies, waits for them, and re-layouts  0.97 us

profile of v3, /device:TPU:0, one launch (start us, length us, event | category | flops | bytes accessed | tf_op | source)
XLA Modules:
  0.0 45.2 jit_solution(13572050967011541345)
XLA Ops:
  0.0 44.2 %shard_map.55 = f32[2048,128]{1,0:T(8,128)S(1)} custom-call(s32[2,6]{1,0:T(2,128)} %bitcast.15, bf16[6,256,256]{2,1,0:T(8,128)(2,1)} %bitcast.11, bf16[256,2,256]{2,1,0:T(2,128)(2,1)} %bitcast.12, bf16[256,2,256]{2,1,0:T(2,128)(2,1)} %bitcast.13, bf16[256,2,256]{2,1,0:T(2,128)(2,1)} %bitcast.14), custom_call_target="tpu_custom_call" | custom-call | tf_op jit(solution)/shard_map/pallas_call | solution.py:544
  44.2 1.0 %copy.8 = f32[1,256,2,2,256]{4,3,2,1,0:T(2,128)} copy(f32[1,256,2,2,256]{4,3,2,1,0:T(2,128)S(1)} %bitcast.10) | data formatting | bytes 2097152

commit v4 on v3

--- a/solution.py
+++ b/solution.py
@@ -329,6 +329,10 @@
         side_copy.wait_recv()
         lax.fori_loop(0, terms // side_group, right_group, 0)
 
+    def right_chunk(n, j):
+        for k in range(terms):
+            h[n, k, lax.rem(j, pairs), block_of(j // pairs)] = matmul(v[j], rbuf[k]).astype(BF16)
+
     def first_right(i, carry):
         level = jnp.where(is_even, own_level + i - 2 * own_level * i, i)
 
@@ -487,9 +491,17 @@
             squares = pass_outward(n, done, squares)
             if n < STEPS - 1:
 
-                @pl.when(lax.rem(done, pairs) == pairs - 1)
+                late = jnp.logical_and(is_end, done >= chunks - pairs)
+
+                @pl.when(
+                    jnp.logical_and(jnp.logical_not(late), lax.rem(done, pairs) == pairs - 1)
+                )
                 def _():
                     right_of(n + 1, done // pairs)
+
+                @pl.when(late)
+                def _():
+                    right_chunk(n + 1, done)
 
             return squares
 

time: 45.3 us -> 45.2 us (level)
  no operation moved by 1% of the time
where the time goes in v4:
time: 45.2 us; the launch traced here: 45.1 us
  Pallas kernels  44.1 us (98%)
  local copies, waits for them, and re-layouts  0.97 us (2%)
    pallas_call x1, Pallas kernels, shards(): pl.pallas_call(functools.partial(kernel, n_sec, n_term, terms), out_shape...  44.1 us
    unnamed x1, local copies, waits for them, and re-layouts  0.97 us

profile of v4, /device:TPU:0, one launch (start us, length us, event | category | flops | bytes accessed | tf_op | source)
XLA Modules:
  0.0 45.1 jit_solution(10754395829502114410)
XLA Ops:
  0.0 44.1 %shard_map.55 = f32[2048,128]{1,0:T(8,128)S(1)} custom-call(s32[2,6]{1,0:T(2,128)} %bitcast.15, bf16[6,256,256]{2,1,0:T(8,128)(2,1)} %bitcast.11, bf16[256,2,256]{2,1,0:T(2,128)(2,1)} %bitcast.12, bf16[256,2,256]{2,1,0:T(2,128)(2,1)} %bitcast.13, bf16[256,2,256]{2,1,0:T(2,128)(2,1)} %bitcast.14), custom_call_target="tpu_custom_call" | custom-call | tf_op jit(solution)/shard_map/pallas_call | solution.py:556
  44.1 1.0 %copy.8 = f32[1,256,2,2,256]{4,3,2,1,0:T(2,128)} copy(f32[1,256,2,2,256]{4,3,2,1,0:T(2,128)S(1)} %bitcast.10) | data formatting | bytes 2097152
